TPU v7x, 32 devices: a whole 2x2x4 slice. The times are simulated.
32 devices in a mesh: row: 4 (over x, core), col: 8 (over z, y).
Axes of the slice: x: 2, y: 2, z: 4, core: 2. Of those that a mesh axis runs over, the one named last changes fastest.
Arguments:
- front_matrix: float32 [32, 4, 128, 16, 8, 128], P(None, 'row', None, None, 'col'), as said below
- children: bfloat16 [2, 4, 4, 128, 16, 8, 128], P(None, None, 'row', None, None, 'col'), may hold values from -0.5 to 0.5
- child_map: int32 [2, 16], replicated, may hold values from 0 to 127, as said below
- row_order: int32 [2, 16, 128], replicated, may hold values from 0 to 127, each once within a row
Outputs:
- schur_part: float32 [32, 4, 128, 16, 8, 128], P(None, 'row', None, None, 'col')
- factor_part: float32 [32, 4, 128, 1536], P('col', 'row')
Inputs may be any that keep to these rules, and one draw needn't show every extreme that they name: `front_matrix`: Off-diagonal entries lie within -1.2 and 1.2 + 0.3 * sqrt(16384); diagonal entries lie between 2.5 and 3.9 times the square root of 16384. The lower triangle, with the children's rows added and mirrored, is positive definite. `child_map`: each child sends its tile rows to distinct front tile rows. Of the 4 tile rows of one child held by one device row, at most 2 go to any one device row (front tile row modulo 4), and exactly 2 go to some device row.
All inputs are finite; a program needn't handle non-finite values.
Results may differ from a plain program's by a relative error of at most 0.001.
Values may be sent and summed in bfloat16 or wider, within the bound.
No kernel may reach another device: no remote copies, remote signals or barrier semaphores. Data moves between devices by JAX's collectives and lax.ppermute only.
A program may use at most 384 MiB of HBM per device.

v0:
```python
import jax
import jax.numpy as jnp
from jax import lax
from jax.sharding import PartitionSpec as P

PWT = 4
STEPS = 3
CAP = 2


def from_root(value, axis, source):
    kept = jnp.where(lax.axis_index(axis) == source, value, 0).astype(value.dtype)
    return lax.psum(kept, axis)


def slot_ranks(mapping, row_count):
    indices = jnp.arange(mapping.shape[0], dtype=jnp.int32)
    sources = indices % row_count
    targets = mapping % row_count
    earlier = (
        (sources[:, None] == sources[None, :])
        & (targets[:, None] == targets[None, :])
        & (indices[None, :] < indices[:, None])
    )
    return (sources, targets, jnp.sum(earlier.astype(jnp.int32), axis=1))


def pack_child(rows_local, ordering, targets, rank_in_group, row_count, row_dev):
    local_count, tile_size, width_local = rows_local.shape
    own_ids = jnp.arange(local_count, dtype=jnp.int32) * row_count + row_dev
    own_order = ordering[own_ids]
    onehot_rows = (
        own_order[:, :, None] == jnp.arange(tile_size, dtype=jnp.int32)[None, None, :]
    ).astype(jnp.bfloat16)
    moved_rows = jnp.einsum(
        "atr,atx->arx", onehot_rows, rows_local, preferred_element_type=jnp.float32
    ).astype(jnp.bfloat16)
    slot_of = targets[own_ids] * CAP + rank_in_group[own_ids]
    selector = (jnp.arange(row_count * CAP, dtype=jnp.int32)[:, None] == slot_of[None, :]).astype(
        jnp.bfloat16
    )
    packed = jnp.einsum(
        "ja,arx->jrx", selector, moved_rows, preferred_element_type=jnp.float32
    ).astype(jnp.bfloat16)
    return packed.reshape(row_count, CAP, tile_size, width_local)


def unpack_selector(mapping, sources, targets, rank_in_group, row_count, row_dev, local_rows):
    slot_of = sources * CAP + rank_in_group
    landing = (
        (mapping // row_count)[:, None] == jnp.arange(local_rows, dtype=jnp.int32)[None, :]
    ) & (targets == row_dev)[:, None]
    arrival = slot_of[:, None] == jnp.arange(row_count * CAP, dtype=jnp.int32)[None, :]
    return jnp.dot(
        landing.astype(jnp.bfloat16).T,
        arrival.astype(jnp.bfloat16),
        preferred_element_type=jnp.float32,
    ).astype(jnp.bfloat16)


def place_rows(matrix_rows, selector, received):
    flat_slots = received.reshape(selector.shape[1], received.shape[2], received.shape[3])
    return matrix_rows + jnp.einsum(
        "aj,jtx->atx", selector, flat_slots, preferred_element_type=jnp.float32
    )


def current_tile(matrix, factors, copies, local_col, tile_size):
    owned = matrix[:, :, local_col * tile_size : (local_col + 1) * tile_size]
    for earlier_index in range(len(factors)):
        owned = owned - jnp.einsum(
            "atk,uk->atu",
            factors[earlier_index],
            copies[earlier_index][local_col],
            precision=lax.Precision.HIGHEST,
            preferred_element_type=jnp.float32,
        )
    return owned


def shards(front_matrix, children, child_map, row_order):
    row_count = lax.axis_size("row")
    col_count = lax.axis_size("col")
    row_dev = lax.axis_index("row")
    col_dev = lax.axis_index("col")
    local_rows = front_matrix.shape[0]
    tile_size = front_matrix.shape[2]
    local_cols = front_matrix.shape[3]
    width_local = local_cols * tile_size
    panel_width = PWT * tile_size
    matrix = front_matrix.reshape(local_rows, tile_size, width_local)
    packed = []
    selectors = []
    for child_index in range(2):
        sources, targets, rank_in_group = slot_ranks(child_map[child_index], row_count)
        rows_local = children[child_index].reshape(children.shape[1], tile_size, width_local)
        packed.append(
            pack_child(
                rows_local, row_order[child_index], targets, rank_in_group, row_count, row_dev
            )
        )
        selectors.append(
            unpack_selector(
                child_map[child_index],
                sources,
                targets,
                rank_in_group,
                row_count,
                row_dev,
                local_rows,
            )
        )
    received = (
        lax.all_to_all(packed[0], "row", split_axis=0, concat_axis=0, tiled=True),
        lax.all_to_all(packed[1], "row", split_axis=0, concat_axis=0, tiled=True),
    )
    for child_index in range(2):
        matrix = place_rows(matrix, selectors[child_index], received[child_index])
    pending = []
    row_tiles = jnp.arange(local_rows, dtype=jnp.int32) * row_count + row_dev
    col_tiles = jnp.arange(local_cols, dtype=jnp.int32) * col_count + col_dev
    factors = []
    copies = []
    for panel_index in range(STEPS):
        first_tile = panel_index * PWT
        pieces = []
        for offset in range(PWT):
            tile_col = first_tile + offset
            local_col = tile_col // col_count
            owned = current_tile(matrix, factors, copies, local_col, tile_size)
            pieces.append(from_root(owned, "col", tile_col % col_count))
        panel_cols = jnp.concatenate(pieces, axis=2)
        blocks = []
        for offset in range(PWT):
            tile_row = first_tile + offset
            blocks.append(from_root(panel_cols[tile_row // row_count], "row", tile_row % row_count))
        diagonal = jnp.concatenate(blocks, axis=0)
        mirrored = jnp.tril(diagonal) + jnp.tril(diagonal, -1).T
        cholesky_factor = jnp.linalg.cholesky(mirrored)
        flat_cols = panel_cols.reshape(local_rows * tile_size, panel_width)
        solved = jax.scipy.linalg.solve_triangular(
            cholesky_factor, flat_cols.T, lower=True
        ).T.reshape(local_rows, tile_size, panel_width)
        diag_rows = cholesky_factor.reshape(PWT, tile_size, panel_width)[
            jnp.clip(row_tiles - first_tile, 0, PWT - 1)
        ]
        inside = (row_tiles >= first_tile) & (row_tiles < first_tile + PWT)
        factor = jnp.where(inside[:, None, None], diag_rows, solved)
        factor = jnp.where((row_tiles < first_tile)[:, None, None], jnp.zeros_like(factor), factor)
        picked = factor[col_tiles // row_count]
        factor_cols = from_root(picked.astype(jnp.bfloat16), "row", col_dev % row_count).astype(
            picked.dtype
        )
        factors.append(factor)
        copies.append(factor_cols)
    stacked = jnp.concatenate(factors, axis=2)
    stacked_cols = jnp.concatenate(copies, axis=2)
    update = jnp.einsum(
        "atk,buk->atbu",
        stacked,
        stacked_cols,
        precision=lax.Precision.HIGHEST,
        preferred_element_type=jnp.float32,
    )
    final_rows = matrix.reshape(local_rows, tile_size, local_cols, tile_size) - update
    kept_mask = (row_tiles[:, None] >= col_tiles[None, :]) & (col_tiles[None, :] >= STEPS * PWT)
    schur_part = jnp.where(
        kept_mask[:, None, :, None], final_rows, jnp.zeros_like(final_rows)
    ).reshape(front_matrix.shape)
    share_rows = local_rows // col_count
    factor_part = lax.dynamic_slice_in_dim(stacked, col_dev * share_rows, share_rows, 0).reshape(
        share_rows, 1, tile_size, STEPS * panel_width
    )
    return (schur_part, factor_part)


def solution(mesh):
    placed = (
        P(None, "row", None, None, "col", None),
        P(None, None, "row", None, None, "col", None),
        P(),
        P(),
    )
    return jax.shard_map(
        shards,
        mesh=mesh,
        in_specs=placed,
        out_specs=(P(None, "row", None, None, "col", None), P("col", "row", None, None)),
        check_vma=False,
    )
```

profile of v0, /device:TPU:0, one launch (start us, length us, event | category | flops | bytes accessed | tf_op | source)
XLA Modules:
  0.0 2242.3 jit_solution(8669075045916751442)
XLA Ops:
  67.1 24.8 %all-to-all-done.1 = bf16[4,2,128,2048]{3,1,2,0:T(2,128)(2,1)} async-done(((bf16[4,2,128,2048]{3,1,2,0:T(2,128)(2,1)}), bf16[4,2,128,2048]{3,1,2,0:T(2,128)(2,1)}, u32[]{:S(2)}, u32[]{:S(2)}) %all-to-all-start.1) | async-done | bytes 4194336 | tf_op jit(solution)/shard_map/all_to_all | solution.py:115
  97.4 92.9 %reduce.19 = f32[32,128,16,128]{3,2,1,0:T(8,128)} reduce(f32[32,1,128,16,1,128]{5,4,3,2,1,0:T(1,128)} %param.7, f32[]{:T(128)} %broadcast.1002), dimensions={1,4}, to_apply=%param.7.reduce_sub_computation.3 | reduce | bytes 67108864 | tf_op args[0]
  190.3 35.5 %reshape.502 = f32[32,128,2048]{2,1,0:T(8,128)} reshape(f32[32,128,16,128]{3,2,1,0:T(8,128)} %reduce.19) | data formatting | bytes 67108864 | tf_op jit(solution)/shard_map/reshape | solution.py:91
  259.0 15.9 fusion.63
  274.9 14.9 fusion.64
  289.8 67.2 %copy_add_fusion = f32[32,128,2048]{2,1,0:T(8,128)} fusion(f32[32,128,2048]{2,0,1:T(8,128)} %fusion.63, f32[32,128,2048]{2,1,0:T(8,128)} %reshape.502, f32[32,128,2048]{2,0,1:T(8,128)} %fusion.64), kind=kLoop, calls=%fused_computation.21 | loop fusion | flops 16777216 | bytes 134217728 | tf_op jit(solution)/shard_map/add | solution.py:63
  362.5 275.0 %all-reduce.27.cloned.1.call-done = (f32[32,128,128]{2,1,0:T(8,128)}, f32[32,128,128]{2,1,0:T(8,128)}, f32[32,128,128]{2,1,0:T(8,128)}, f32[32,128,128]{2,1,0:T(8,128)}) async-done(((f32[32,128,128]{2,1,0:T(8,128)}, f32[32,128,128]{2,1,0:T(8,128)}, f32[32,128,128]{2,1,0:T(8,128)}, f32[32,128,128]{2,1,0:T(8,128)}), (f32[32,128,128]{2,1,0:T(8,128)}, f32[32,128,128]{2,1,0:T(8,128)}, f32[32,128,128]{2,1,0:T(8,128)}, ...) | async-done | bytes 8388624 | tf_op jit(solution)/shard_map/psum | solution.py:13
  657.0 26.2 %all-reduce.33.cloned.1.call-done = (f32[128,512]{1,0:T(8,128)}, f32[128,512]{1,0:T(8,128)}, f32[128,512]{1,0:T(8,128)}, f32[128,512]{1,0:T(8,128)}) async-done(((f32[128,512]{1,0:T(8,128)}, f32[128,512]{1,0:T(8,128)}, f32[128,512]{1,0:T(8,128)}, f32[128,512]{1,0:T(8,128)}), (f32[128,512]{1,0:T(8,128)}, f32[128,512]{1,0:T(8,128)}, f32[128,512]{1,0:T(8,128)}, ...) | async-done | bytes 1048592 | tf_op jit(solution)/shard_map/psum | solution.py:13
  688.2 11.7 cholesky.374
  710.5 11.7 cholesky.393
  733.2 11.7 cholesky.414
  755.4 11.8 cholesky.431
  794.4 39.3 %custom-call.34 = f32[4,128,128]{1,2,0:T(8,128)S(1)} custom-call(f32[4,128,128]{2,1,0:T(8,128)S(1)} %get-tuple-element.24), custom_call_target="InvertDiagBlocksLowerTriangular" | custom-call | tf_op jit(solution)/shard_map/jit(_solve_triangular)/triangular_solve | solution.py:141
  871.9 11.8 select_select_fusion.4
  911.0 32.4 %all-reduce.17.cloned.1.call-done = bf16[16,128,512]{2,1,0:T(8,128)(2,1)} async-done(((bf16[16,128,512]{2,1,0:T(8,128)(2,1)}), bf16[16,128,512]{2,1,0:T(8,128)(2,1)}) %all-reduce.17.cloned.1.call-update) | async-done | bytes 2097168 | tf_op jit(solution)/shard_map/psum | solution.py:13
  954.9 272.6 %all-reduce.25.cloned.1.call-done = (f32[32,128,128]{2,1,0:T(8,128)}, f32[32,128,128]{2,1,0:T(8,128)}, f32[32,128,128]{2,1,0:T(8,128)}, f32[32,128,128]{2,1,0:T(8,128)}) async-done(((f32[32,128,128]{2,1,0:T(8,128)}, f32[32,128,128]{2,1,0:T(8,128)}, f32[32,128,128]{2,1,0:T(8,128)}, f32[32,128,128]{2,1,0:T(8,128)}), (f32[32,128,128]{2,1,0:T(8,128)}, f32[32,128,128]{2,1,0:T(8,128)}, f32[32,128,128]{2,1,0:T(8,128)}, ...) | async-done | bytes 8388624 | tf_op jit(solution)/shard_map/psum | solution.py:13
  1255.3 17.9 all-reduce.31.cloned.1.call-done
  1278.2 11.7 cholesky.446
  1300.6 11.7 cholesky.465
  1323.2 11.7 cholesky.486
  1345.3 11.9 cholesky.503
  1384.2 39.3 %custom-call.38 = f32[4,128,128]{1,2,0:T(8,128)S(1)} custom-call(f32[4,128,128]{2,1,0:T(8,128)S(1)} %get-tuple-element.25), custom_call_target="InvertDiagBlocksLowerTriangular" | custom-call | tf_op jit(solution)/shard_map/jit(_solve_triangular)/triangular_solve | solution.py:141
  1461.8 12.0 select_select_fusion.2
  1500.1 33.3 %all-reduce.19.cloned.1.call-done = bf16[16,128,512]{2,1,0:T(8,128)(2,1)} async-done(((bf16[16,128,512]{2,1,0:T(8,128)(2,1)}), bf16[16,128,512]{2,1,0:T(8,128)(2,1)}) %all-reduce.19.cloned.1.call-update) | async-done | bytes 2097168 | tf_op jit(solution)/shard_map/psum | solution.py:13
  1545.3 272.2 %all-reduce.23.cloned.1.call-done = (f32[32,128,128]{2,1,0:T(8,128)}, f32[32,128,128]{2,1,0:T(8,128)}, f32[32,128,128]{2,1,0:T(8,128)}, f32[32,128,128]{2,1,0:T(8,128)}) async-done(((f32[32,128,128]{2,1,0:T(8,128)}, f32[32,128,128]{2,1,0:T(8,128)}, f32[32,128,128]{2,1,0:T(8,128)}, f32[32,128,128]{2,1,0:T(8,128)}), (f32[32,128,128]{2,1,0:T(8,128)}, f32[32,128,128]{2,1,0:T(8,128)}, f32[32,128,128]{2,1,0:T(8,128)}, ...) | async-done | bytes 8388624 | tf_op jit(solution)/shard_map/psum | solution.py:13
  1837.0 26.2 %all-reduce.29.cloned.1.call-done = (f32[128,512]{1,0:T(8,128)}, f32[128,512]{1,0:T(8,128)}, f32[128,512]{1,0:T(8,128)}, f32[128,512]{1,0:T(8,128)}) async-done(((f32[128,512]{1,0:T(8,128)}, f32[128,512]{1,0:T(8,128)}, f32[128,512]{1,0:T(8,128)}, f32[128,512]{1,0:T(8,128)}), (f32[128,512]{1,0:T(8,128)}, f32[128,512]{1,0:T(8,128)}, f32[128,512]{1,0:T(8,128)}, ...) | async-done | bytes 1048592 | tf_op jit(solution)/shard_map/psum | solution.py:13
  1935.5 11.9 cholesky.575
  1960.9 39.3 %custom-call.42 = f32[4,128,128]{1,2,0:T(8,128)S(1)} custom-call(f32[4,128,128]{2,1,0:T(8,128)S(1)} %get-tuple-element.26), custom_call_target="InvertDiagBlocksLowerTriangular" | custom-call | tf_op jit(solution)/shard_map/jit(_solve_triangular)/triangular_solve | solution.py:141
  2040.2 12.1 select_select_fusion
  2069.7 40.1 %all-reduce.21.cloned.1.call-done = bf16[16,128,512]{2,1,0:T(8,128)(2,1)} async-done(((bf16[16,128,512]{2,1,0:T(8,128)(2,1)}), bf16[16,128,512]{2,1,0:T(8,128)(2,1)}) %all-reduce.21.cloned.1.call-update) | async-done | bytes 2097168 | tf_op jit(solution)/shard_map/psum | solution.py:13
  2109.8 87.0 %fusion.1 = f32[32,1,128,16,1,128]{5,2,3,0,4,1:T(8,128)} fusion(pred[32,16]{1,0:T(8,128)(4,1)S(1)} %compare_and_fusion, bf16[16,128,512]{2,1,0:T(8,128)(2,1)} %all-reduce.21.cloned.1.call-done, bf16[16,128,512]{2,1,0:T(8,128)(2,1)} %all-reduce.19.cloned.1.call-done, bf16[16,128,512]{2,1,0:T(8,128)(2,1)S(1)} %copy-done.19, ...), kind=kOutput, calls=%fused_computation.20 | convolution fusion | flops 154667057152 | bytes 98566656 | tf_op jit(solution)/shard_map/atk,buk->atbu/dot_general | solution.py:158
  2196.8 38.6 %copy.107 = f32[32,1,128,16,1,128]{5,4,3,2,1,0:T(1,128)} copy(f32[32,1,128,16,1,128]{5,2,3,0,4,1:T(8,128)} %fusion.1) | data formatting | bytes 67108864
  (323 shorter events, 611.0 us)
Async XLA Ops:
  13.7 2.8 copy-start.20
  38.0 53.9 %all-to-all-start.1 = ((bf16[4,2,128,2048]{3,1,2,0:T(2,128)(2,1)}), bf16[4,2,128,2048]{3,1,2,0:T(2,128)(2,1)}, u32[]{:S(2)}, u32[]{:S(2)}) async-start(bf16[4,2,128,2048]{3,1,2,0:T(2,128)(2,1)} %copy.83), calls=%async_computation.1 | async-start | bytes 8388608 | tf_op jit(solution)/shard_map/all_to_all | solution.py:115
  91.9 150.5 %all-to-all-start = ((bf16[4,2,128,2048]{3,1,2,0:T(2,128)(2,1)}), bf16[4,2,128,2048]{3,1,2,0:T(2,128)(2,1)}, u32[]{:S(2)}, u32[]{:S(2)}) async-start(bf16[4,2,128,2048]{3,1,2,0:T(2,128)(2,1)} %copy.79), calls=%async_computation | async-start | bytes 8388608 | tf_op jit(solution)/shard_map/all_to_all | solution.py:114
  96.8 540.7 %all-reduce.27.cloned.1.call-start = ((), (), s32[]{:S(2)}) async-start(), calls=%async_computation.7 | async-start | bytes 16777216 | tf_op jit(solution)/shard_map/psum | solution.py:13
  190.3 35.5 %copy-start.21 = (s32[2,16]{1,0:T(2,128)S(1)}, s32[2,16]{1,0:T(2,128)}, u32[]{:S(2)}) copy-start(s32[2,16]{1,0:T(2,128)} %param.9) | copy-start | bytes 388
  362.3 320.8 %all-reduce.33.cloned.1.call-start = ((), (), s32[]{:S(2)}) async-start(), calls=%async_computation.10 | async-start | bytes 2097152 | tf_op jit(solution)/shard_map/psum | solution.py:13
  637.5 2.2 copy-start.12
  639.7 1.6 copy-start.11
  641.3 1.6 copy-start.10
  643.2 3.4 copy-start.6
  647.6 295.8 %all-reduce.17.cloned.1.call-start = ((), (), s32[]{:S(2)}) async-start(), calls=%async_computation.2 | async-start | bytes 4194304 | tf_op jit(solution)/shard_map/psum | solution.py:13
  842.7 15.1 copy-start
  849.4 8.5 copy-start.2
  857.9 1.3 copy-start.4
  892.2 335.3 %all-reduce.25.cloned.1.call-start = ((), (), s32[]{:S(2)}) async-start(), calls=%async_computation.6 | async-start | bytes 16777216 | tf_op jit(solution)/shard_map/psum | solution.py:13
  954.7 318.5 %all-reduce.31.cloned.1.call-start = ((), (), s32[]{:S(2)}) async-start(), calls=%async_computation.9 | async-start | bytes 2097152 | tf_op jit(solution)/shard_map/psum | solution.py:13
  1227.5 2.2 copy-start.18
  1229.7 1.6 copy-start.17
  1231.3 1.6 copy-start.16
  1233.2 3.4 copy-start.7
  1237.6 295.8 %all-reduce.19.cloned.1.call-start = ((), (), s32[]{:S(2)}) async-start(), calls=%async_computation.3 | async-start | bytes 4194304 | tf_op jit(solution)/shard_map/psum | solution.py:13
  1432.5 15.3 copy-start.1
  1439.2 8.6 copy-start.3
  1482.3 335.3 %all-reduce.23.cloned.1.call-start = ((), (), s32[]{:S(2)}) async-start(), calls=%async_computation.5 | async-start | bytes 16777216 | tf_op jit(solution)/shard_map/psum | solution.py:13
  1490.9 42.6 %copy-start.9 = (f32[32,128,128]{2,1,0:T(8,128)S(1)}, f32[32,128,128]{2,1,0:T(8,128)}, u32[]{:S(2)}) copy-start(f32[32,128,128]{2,1,0:T(8,128)} %fusion.83) | copy-start | bytes 6291460
  1544.7 318.5 %all-reduce.29.cloned.1.call-start = ((), (), s32[]{:S(2)}) async-start(), calls=%async_computation.8 | async-start | bytes 2097152 | tf_op jit(solution)/shard_map/psum | solution.py:13
  1817.5 2.2 copy-start.15
  1819.8 1.6 copy-start.14
  1821.3 1.6 copy-start.13
  1823.2 3.4 copy-start.8
  1827.6 282.1 %all-reduce.21.cloned.1.call-start = ((), (), s32[]{:S(2)}) async-start(), calls=%async_computation.4 | async-start | bytes 4194304 | tf_op jit(solution)/shard_map/psum | solution.py:13
  2067.8 42.0 %copy-start.19 = (bf16[16,128,512]{2,1,0:T(8,128)(2,1)S(1)}, bf16[16,128,512]{2,1,0:T(8,128)(2,1)}, u32[]{:S(2)}) copy-start(bf16[16,128,512]{2,1,0:T(8,128)(2,1)} %all-reduce.17.cloned.1.call-done) | copy-start | bytes 6291460
  (1 other events, 1.3 us)
Sparse Core Ops, SparseCore 0:
  362.4 274.9 all-reduce.26
  647.7 35.3 all-reduce.32
  892.4 51.0 all-reduce.16
  954.8 272.6 all-reduce.24
  1237.7 35.3 all-reduce.30
  1482.4 51.0 all-reduce.18
  1544.9 272.6 all-reduce.22
  1827.8 35.3 all-reduce.28
  2058.0 51.7 all-reduce.20
where the time goes:
time: 2250 us; the launch traced here: 2240 us
  waiting for transfers between devices  1020 us (45%)
  other arithmetic  612 us (27%)
  local copies, waits for them, and re-layouts  342 us (15%)
  matrix products  234 us (10%)
  between operations  23.2 us (1%)
    psum x9, waiting for transfers between devices, from_root(): return lax.psum(kept, axis)  996 us
    another operation x45, other arithmetic, shards(): cholesky_factor = jnp.linalg.cholesky(mirrored)  239 us
    another operation x7, other arithmetic, shards(): jax.scipy.linalg.solve_triangular(cholesky_factor, flat_cols.T, lower=True)  119 us
    unnamed x1, other arithmetic  92.9 us
    dot_general x1, matrix products, shards(): jnp.einsum('atk,buk->atbu', stacked, stacked_cols, precision=lax.Precisio...  87 us
    unnamed x64, local copies, waits for them, and re-layouts  76.8 us
    another operation x21, matrix products, shards(): jax.scipy.linalg.solve_triangular(cholesky_factor, flat_cols.T, lower=True)  70.8 us
    add x1, other arithmetic, place_rows(): matrix_rows + jnp.einsum('aj,jtx->atx', selector, flat_slots, preferred_e...  67.2 us
  transfers between devices with their start and end apart: 11, of which 10 were waited for; matrix products, arithmetic and copies ran while one was open for 11% of the time, Pallas kernels for 0%

commit v1 on v0

--- a/solution.py
+++ b/solution.py
@@ -10,7 +10,7 @@
 
 def from_root(value, axis, source):
     kept = jnp.where(lax.axis_index(axis) == source, value, 0).astype(value.dtype)
-    return lax.psum(kept, axis)
+    return jnp.sum(lax.all_gather(kept, axis), axis=0)
 
 
 def slot_ranks(mapping, row_count):

time: 2250 us -> 4290 us (1.91)
  waiting for transfers between devices: 1020 us -> 2860 us
  other arithmetic: 612 us -> 700 us
  local copies, waits for them, and re-layouts: 342 us -> 409 us
    all_gather x0 -> x27, waiting for transfers between devices: none -> 2830 us  [from_root(): return jnp.sum(lax.all_gather(kept, axis), axis=0)]
    psum x9 -> x0, waiting for transfers between devices: 996 us -> none  [from_root(): return lax.psum(kept, axis)]
    reduce_sum x0 -> x27, other arithmetic: none -> 148 us  [from_root(): return jnp.sum(lax.all_gather(kept, axis), axis=0)]
    add x1 -> x0, other arithmetic: 67.2 us -> none  [place_rows(): matrix_rows + jnp.einsum('aj,jtx->atx', selector, flat_slots, preferred_e...]
    unnamed x64 -> x37, local copies, waits for them, and re-layouts: 76.8 us -> 129 us
    unnamed x1 -> x2, other arithmetic: 92.9 us -> 100 us
  transfers between devices with their start and end apart: 11 -> 29, of which waited for: 10 -> 25; matrix products, arithmetic and copies ran while one was open for 11% -> 11% of each run, Pallas kernels for 0% -> 0%
where the time goes in v1:
time: 4290 us; the launch traced here: 4280 us
  waiting for transfers between devices  2860 us (67%)
  other arithmetic  700 us (16%)
  local copies, waits for them, and re-layouts  409 us (10%)
  matrix products  276 us (6%)
    all_gather x27, waiting for transfers between devices, from_root(): return jnp.sum(lax.all_gather(kept, axis), axis=0)  2830 us
    another operation x45, other arithmetic, shards(): cholesky_factor = jnp.linalg.cholesky(mirrored)  239 us
    reduce_sum x27, other arithmetic, from_root(): return jnp.sum(lax.all_gather(kept, axis), axis=0)  148 us
    unnamed x37, local copies, waits for them, and re-layouts  129 us
    another operation x7, other arithmetic, shards(): jax.scipy.linalg.solve_triangular(cholesky_factor, flat_cols.T, lower=True)  119 us
    unnamed x2, other arithmetic  100 us
    dot_general x1, matrix products, shards(): jnp.einsum('atk,buk->atbu', stacked, stacked_cols, precision=lax.Precisio...  94.6 us
  transfers between devices with their start and end apart: 29, of which 25 were waited for; matrix products, arithmetic and copies ran while one was open for 11% of the time, Pallas kernels for 0%

profile of v1, /device:TPU:0, one launch (start us, length us, event | category | flops | bytes accessed | tf_op | source)
XLA Modules:
  0.0 4276.8 jit_solution(11598522297085850806)
XLA Ops:
  67.8 24.8 all-to-all-done
  98.0 92.7 %reduce.22 = f32[32,128,16,128]{3,2,1,0:T(8,128)} reduce(f32[32,1,128,16,1,128]{5,4,3,2,1,0:T(1,128)} %param.7, f32[]{:T(128)} %broadcast.1047), dimensions={1,4}, to_apply=%param.7.reduce_sub_computation.3 | reduce | bytes 67108864 | tf_op args[0]
  190.7 35.5 reshape.670
  259.4 15.9 fusion.71
  275.3 43.2 %fusion = f32[32,128,2048]{2,0,1:T(8,128)} fusion(f32[32,128,2048]{2,0,1:T(8,128)} %fusion.71, f32[32,128,2048]{2,1,0:T(8,128)} %reshape.670, bf16[8,128,2048]{2,0,1:T(8,128)(2,1)} %reshape.512, s32[16]{0:T(128)S(1)} %multiply_add_fusion.5, s32[16]{0:T(128)S(1)} %get-tuple-element.139, pred[16]{0:T(512)(128)(4,1)S(1)} %get-tuple-element.141), kind=kOutput, calls=%fused_computation.19 | convolution fusion | flops 151004544 | bytes 104857744 | tf_op jit(solution)/shard_map/aj,jtx->atx/dot_general | solution.py:63
  326.1 228.0 %all-gather.67.cloned.1.call-done = f32[256,128,128]{2,0,1:T(8,128)} async-done(((f32[32,128,128]{2,0,1:T(8,128)}), f32[256,128,128]{2,0,1:T(8,128)}) %all-gather.67.cloned.1.call-update) | async-done | bytes 16777232 | tf_op jit(solution)/shard_map/all_gather | solution.py:13
  562.5 219.6 %all-gather.69.cloned.1.call-done = f32[256,128,128]{2,0,1:T(8,128)} async-done(((f32[32,128,128]{2,0,1:T(8,128)}), f32[256,128,128]{2,0,1:T(8,128)}) %all-gather.69.cloned.1.call-update) | async-done | bytes 16777232 | tf_op jit(solution)/shard_map/all_gather | solution.py:13
  791.8 218.3 %all-gather.71.cloned.1.call-done = f32[256,128,128]{2,0,1:T(8,128)} async-done(((f32[32,128,128]{2,0,1:T(8,128)}), f32[256,128,128]{2,0,1:T(8,128)}) %all-gather.71.cloned.1.call-update) | async-done | bytes 16777232 | tf_op jit(solution)/shard_map/all_gather | solution.py:13
  1019.9 218.0 %all-gather.73.cloned.1.call-done = f32[256,128,128]{2,0,1:T(8,128)} async-done(((f32[32,128,128]{2,0,1:T(8,128)}), f32[256,128,128]{2,0,1:T(8,128)}) %all-gather.73.cloned.1.call-update) | async-done | bytes 16777232 | tf_op jit(solution)/shard_map/all_gather | solution.py:13
  1290.1 17.0 all-gather.47.cloned.1.call-done
  1308.4 17.6 all-gather.49.cloned.1.call-done
  1421.4 39.5 custom-call.34
  1556.7 25.7 all-gather.75.cloned.1.call-done
  1601.8 225.5 %all-gather.77.cloned.1.call-done = f32[256,128,128]{2,0,1:T(8,128)} async-done(((f32[32,128,128]{2,0,1:T(8,128)}), f32[256,128,128]{2,0,1:T(8,128)}) %all-gather.77.cloned.1.call-update) | async-done | bytes 16777232 | tf_op jit(solution)/shard_map/all_gather | solution.py:13
  1835.7 219.6 %all-gather.79.cloned.1.call-done = f32[256,128,128]{2,0,1:T(8,128)} async-done(((f32[32,128,128]{2,0,1:T(8,128)}), f32[256,128,128]{2,0,1:T(8,128)}) %all-gather.79.cloned.1.call-update) | async-done | bytes 16777232 | tf_op jit(solution)/shard_map/all_gather | solution.py:13
  2065.1 218.0 %all-gather.81.cloned.1.call-done = f32[256,128,128]{2,0,1:T(8,128)} async-done(((f32[32,128,128]{2,0,1:T(8,128)}), f32[256,128,128]{2,0,1:T(8,128)}) %all-gather.81.cloned.1.call-update) | async-done | bytes 16777232 | tf_op jit(solution)/shard_map/all_gather | solution.py:13
  2292.9 218.2 %all-gather.83.cloned.1.call-done = f32[256,128,128]{2,0,1:T(8,128)} async-done(((f32[32,128,128]{2,0,1:T(8,128)}), f32[256,128,128]{2,0,1:T(8,128)}) %all-gather.83.cloned.1.call-update) | async-done | bytes 16777232 | tf_op jit(solution)/shard_map/all_gather | solution.py:13
  2563.6 16.7 all-gather.55.cloned.1.call-done
  2581.8 17.3 all-gather.57.cloned.1.call-done
  2695.6 39.5 custom-call.38
  2834.1 22.7 all-gather.85.cloned.1.call-done
  2882.0 225.2 %all-gather.87.cloned.1.call-done = f32[256,128,128]{2,0,1:T(8,128)} async-done(((f32[32,128,128]{2,0,1:T(8,128)}), f32[256,128,128]{2,0,1:T(8,128)}) %all-gather.87.cloned.1.call-update) | async-done | bytes 16777232 | tf_op jit(solution)/shard_map/all_gather | solution.py:13
  3115.7 219.4 %all-gather.89.cloned.1.call-done = f32[256,128,128]{2,0,1:T(8,128)} async-done(((f32[32,128,128]{2,0,1:T(8,128)}), f32[256,128,128]{2,0,1:T(8,128)}) %all-gather.89.cloned.1.call-update) | async-done | bytes 16777232 | tf_op jit(solution)/shard_map/all_gather | solution.py:13
  3344.9 218.2 %all-gather.91.cloned.1.call-done = f32[256,128,128]{2,0,1:T(8,128)} async-done(((f32[32,128,128]{2,0,1:T(8,128)}), f32[256,128,128]{2,0,1:T(8,128)}) %all-gather.91.cloned.1.call-update) | async-done | bytes 16777232 | tf_op jit(solution)/shard_map/all_gather | solution.py:13
  3572.9 218.2 %all-gather.93.cloned.1.call-done = f32[256,128,128]{2,0,1:T(8,128)} async-done(((f32[32,128,128]{2,0,1:T(8,128)}), f32[256,128,128]{2,0,1:T(8,128)}) %all-gather.93.cloned.1.call-update) | async-done | bytes 16777232 | tf_op jit(solution)/shard_map/all_gather | solution.py:13
  3843.4 17.0 all-gather.63.cloned.1.call-done
  3861.7 17.4 all-gather.65.cloned.1.call-done
  3974.4 39.7 custom-call.42
  4071.2 27.9 copy.323
  4110.8 18.8 all-gather.95.cloned.1.call-done
  4136.5 94.6 %fusion.2 = f32[32,1,128,16,1,128]{5,2,3,0,4,1:T(8,128)} fusion(f32[32,128,16,128]{3,2,0,1:T(8,128)} %bitcast.353, pred[32,16]{1,0:T(8,128)(4,1)S(1)} %compare_and_fusion, bf16[16,128,512]{2,1,0:T(8,128)(2,1)} %reduce_sum.298, bf16[16,128,512]{2,1,0:T(8,128)(2,1)} %reduce_sum.289, bf16[16,128,512]{2,1,0:T(8,128)(2,1)S(1)} %copy-done.13, ...), kind=kOutput, calls=%fused_computation.22 | convolution fusion | flops 154667057152 | bytes 98566656 | tf_op jit(solution)/shard_map/atk,buk->atbu/dot_general | solution.py:158
  4231.1 38.6 copy.261
  (400 shorter events, 969.2 us)
Async XLA Ops:
  38.7 53.9 %all-to-all-start = ((bf16[4,2,128,2048]{3,1,2,0:T(2,128)(2,1)}), bf16[4,2,128,2048]{3,1,2,0:T(2,128)(2,1)}, u32[]{:S(2)}, u32[]{:S(2)}) async-start(bf16[4,2,128,2048]{3,1,2,0:T(2,128)(2,1)} %copy.202), calls=%async_computation | async-start | bytes 8388608 | tf_op jit(solution)/shard_map/all_to_all | solution.py:114
  92.6 150.3 %all-to-all-start.1 = ((bf16[4,2,128,2048]{3,1,2,0:T(2,128)(2,1)}), bf16[4,2,128,2048]{3,1,2,0:T(2,128)(2,1)}, u32[]{:S(2)}, u32[]{:S(2)}) async-start(bf16[4,2,128,2048]{3,1,2,0:T(2,128)(2,1)} %copy.205), calls=%async_computation.1 | async-start | bytes 8388608 | tf_op jit(solution)/shard_map/all_to_all | solution.py:115
  97.4 456.6 %all-gather.67.cloned.1.call-start = ((), (), s32[]{:S(2)}) async-start(), calls=%async_computation.14 | async-start | bytes 18874368 | tf_op jit(solution)/shard_map/all_gather | solution.py:13
  190.7 35.5 copy-start.14
  323.8 458.3 %all-gather.69.cloned.1.call-start = ((), (), s32[]{:S(2)}) async-start(), calls=%async_computation.15 | async-start | bytes 18874368 | tf_op jit(solution)/shard_map/all_gather | solution.py:13
  324.5 685.5 %all-gather.71.cloned.1.call-start = ((), (), s32[]{:S(2)}) async-start(), calls=%async_computation.16 | async-start | bytes 18874368 | tf_op jit(solution)/shard_map/all_gather | solution.py:13
  325.3 912.6 %all-gather.73.cloned.1.call-start = ((), (), s32[]{:S(2)}) async-start(), calls=%async_computation.17 | async-start | bytes 18874368 | tf_op jit(solution)/shard_map/all_gather | solution.py:13
  325.9 958.3 %all-gather.43.cloned.1.call-start = ((), (), s32[]{:S(2)}) async-start(), calls=%async_computation.2 | async-start | bytes 1310720 | tf_op jit(solution)/shard_map/all_gather | solution.py:13
  1255.5 33.2 all-gather.45.cloned.1.call-start
  1256.3 50.8 %all-gather.47.cloned.1.call-start = ((), (), s32[]{:S(2)}) async-start(), calls=%async_computation.4 | async-start | bytes 1310720 | tf_op jit(solution)/shard_map/all_gather | solution.py:13
  1257.1 68.9 %all-gather.49.cloned.1.call-start = ((), (), s32[]{:S(2)}) async-start(), calls=%async_computation.5 | async-start | bytes 1310720 | tf_op jit(solution)/shard_map/all_gather | solution.py:13
  1257.9 324.5 %all-gather.75.cloned.1.call-start = ((), (), s32[]{:S(2)}) async-start(), calls=%async_computation.18 | async-start | bytes 10485760 | tf_op jit(solution)/shard_map/all_gather | solution.py:13
  1421.4 39.5 copy-start.10
  1524.0 303.2 %all-gather.77.cloned.1.call-start = ((), (), s32[]{:S(2)}) async-start(), calls=%async_computation.19 | async-start | bytes 18874368 | tf_op jit(solution)/shard_map/all_gather | solution.py:13
  1599.5 455.8 %all-gather.79.cloned.1.call-start = ((), (), s32[]{:S(2)}) async-start(), calls=%async_computation.20 | async-start | bytes 18874368 | tf_op jit(solution)/shard_map/all_gather | solution.py:13
  1600.3 682.9 %all-gather.81.cloned.1.call-start = ((), (), s32[]{:S(2)}) async-start(), calls=%async_computation.21 | async-start | bytes 18874368 | tf_op jit(solution)/shard_map/all_gather | solution.py:13
  1600.9 910.3 %all-gather.83.cloned.1.call-start = ((), (), s32[]{:S(2)}) async-start(), calls=%async_computation.22 | async-start | bytes 18874368 | tf_op jit(solution)/shard_map/all_gather | solution.py:13
  1601.6 956.1 %all-gather.51.cloned.1.call-start = ((), (), s32[]{:S(2)}) async-start(), calls=%async_computation.6 | async-start | bytes 1310720 | tf_op jit(solution)/shard_map/all_gather | solution.py:13
  2528.9 33.2 all-gather.53.cloned.1.call-start
  2529.7 50.6 %all-gather.55.cloned.1.call-start = ((), (), s32[]{:S(2)}) async-start(), calls=%async_computation.8 | async-start | bytes 1310720 | tf_op jit(solution)/shard_map/all_gather | solution.py:13
  2530.5 68.5 %all-gather.57.cloned.1.call-start = ((), (), s32[]{:S(2)}) async-start(), calls=%async_computation.9 | async-start | bytes 1310720 | tf_op jit(solution)/shard_map/all_gather | solution.py:13
  2531.3 325.5 %all-gather.85.cloned.1.call-start = ((), (), s32[]{:S(2)}) async-start(), calls=%async_computation.23 | async-start | bytes 10485760 | tf_op jit(solution)/shard_map/all_gather | solution.py:13
  2695.6 39.5 copy-start.11
  2798.5 308.8 %all-gather.87.cloned.1.call-start = ((), (), s32[]{:S(2)}) async-start(), calls=%async_computation.24 | async-start | bytes 18874368 | tf_op jit(solution)/shard_map/all_gather | solution.py:13
  2879.5 455.6 %all-gather.89.cloned.1.call-start = ((), (), s32[]{:S(2)}) async-start(), calls=%async_computation.25 | async-start | bytes 18874368 | tf_op jit(solution)/shard_map/all_gather | solution.py:13
  2880.1 683.0 %all-gather.91.cloned.1.call-start = ((), (), s32[]{:S(2)}) async-start(), calls=%async_computation.26 | async-start | bytes 18874368 | tf_op jit(solution)/shard_map/all_gather | solution.py:13
  2880.8 910.3 %all-gather.93.cloned.1.call-start = ((), (), s32[]{:S(2)}) async-start(), calls=%async_computation.27 | async-start | bytes 18874368 | tf_op jit(solution)/shard_map/all_gather | solution.py:13
  2881.6 956.2 %all-gather.59.cloned.1.call-start = ((), (), s32[]{:S(2)}) async-start(), calls=%async_computation.10 | async-start | bytes 1310720 | tf_op jit(solution)/shard_map/all_gather | solution.py:13
  3808.8 33.2 all-gather.61.cloned.1.call-start
  3809.6 50.8 %all-gather.63.cloned.1.call-start = ((), (), s32[]{:S(2)}) async-start(), calls=%async_computation.12 | async-start | bytes 1310720 | tf_op jit(solution)/shard_map/all_gather | solution.py:13
  3810.4 68.7 %all-gather.65.cloned.1.call-start = ((), (), s32[]{:S(2)}) async-start(), calls=%async_computation.13 | async-start | bytes 1310720 | tf_op jit(solution)/shard_map/all_gather | solution.py:13
  3811.2 318.4 %all-gather.95.cloned.1.call-start = ((), (), s32[]{:S(2)}) async-start(), calls=%async_computation.28 | async-start | bytes 10485760 | tf_op jit(solution)/shard_map/all_gather | solution.py:13
  (12 other events, 86.5 us)
Sparse Core Ops, SparseCore 0:
  323.9 230.0 all-gather.66
  556.2 225.7 all-gather.68
  784.2 225.7 all-gather.70
  1012.1 225.7 all-gather.72
  1255.6 14.8 all-gather.42
  1272.0 16.7 all-gather.44
  1290.3 16.7 all-gather.46
  1309.2 16.7 all-gather.48
  1524.2 58.1 all-gather.74
  1599.7 227.5 all-gather.76
  1829.5 225.7 all-gather.78
  2057.3 225.7 all-gather.80
  2285.3 225.7 all-gather.82
  2529.0 14.8 all-gather.50
  2545.4 16.7 all-gather.52
  2563.6 16.7 all-gather.54
  2582.3 16.7 all-gather.56
  2798.6 58.1 all-gather.84
  2879.6 227.5 all-gather.86
  3109.3 225.7 all-gather.88
  3337.3 225.7 all-gather.90
  3565.3 225.7 all-gather.92
  3808.9 14.8 all-gather.58
  3825.3 16.7 all-gather.60
  3843.6 16.7 all-gather.62
  3862.3 16.7 all-gather.64
  4071.2 58.2 all-gather.94
